TPU v7x, 128 devices: a whole 4x4x4 slice. The times are simulated.
128 devices in a mesh: wave: 8 (over x, core), deg: 16 (over z, y).
Axes of the slice: x: 4, y: 4, z: 4, core: 2. Of those that a mesh axis runs over, the one named last changes fastest.
Arguments:
- spectrum: bfloat16 [512, 2, 32, 4096], P('wave', None, None, 'deg'), may hold values from -2 to 2
- leaf_map: bfloat16 [512, 4096, 128], P('wave', 'deg'), may hold values from -0.375 to 0.375
- level_maps: bfloat16 [3, 512, 2048, 128], P(None, 'wave', 'deg'), may hold values from -0.5 to 0.5
- lat_map: bfloat16 [512, 128, 2048], P('wave', None, 'deg'), may hold values from -0.0234375 to 0.0234375
- skeleton: int32 [512, 2048], P('wave', 'deg'), may hold values from 0 to 255
- wavemap: int32 [512], replicated, may hold values from 0 to 4095, as said below
Outputs:
- grid: bfloat16 [32, 2048, 8192], P('wave', 'deg')
Inputs may be any that keep to these rules, and one draw needn't show every extreme that they name: `skeleton`: for slot m and block b, entries b * 128 to b * 128 + 127 are degrees counted from the first degree of block b. `wavemap`: no two slots hold the same wavenumber.
All inputs are finite; a program needn't handle non-finite values.
Results may differ from a plain program's by a relative error of at most 0.0086.
Values may be sent and summed in bfloat16 or wider, within the bound.
A program may use at most 128 MiB of HBM per device.

v0:
```python
import functools

import jax
import jax.numpy as jnp
from jax import lax
from jax.experimental import pallas as pl
from jax.experimental.pallas import tpu as pltpu
from jax.sharding import PartitionSpec as P

NLON = 8192
LEVELS = 3
SLOTS = 64
CHUNK = 8
CHUNKS = SLOTS // CHUNK
PAIRS = CHUNK // 2
COLS = 64
NODE = 128
WAVE = 8
LON_TILE = 256
LON_TILES = NLON // LON_TILE
MESH = pl.DeviceIdType.MESH
DELAY = (2, 1, 1, 1)


def comm_kernel(
    spec_hbm, leaf_hbm, lev_hbm, lat_hbm, skel_ref, wm_ref,
    xt_ref, t_hbm,
    spec_v, leaf_v, lev_v, lat_v, state, send, recv, lat32, a_send, a_recv, t_v, q_v,
    spec_sem, leaf_sem, lev_sem, lat_sem, t_sem, l_ssem, l_rsem, a_ssem, a_rsem,
):
    me_w = lax.axis_index("wave")
    me_d = lax.axis_index("deg")
    lane_half = lax.broadcasted_iota(jnp.int32, (COLS, NODE), 1) // (NODE // 2)

    def spec_load(c):
        rows = pl.ds(c * CHUNK, CHUNK)
        return pltpu.make_async_copy(spec_hbm.at[rows], spec_v.at[rows], spec_sem.at[c])

    def leaf_load(c):
        rows = pl.ds(c * CHUNK, CHUNK)
        return pltpu.make_async_copy(leaf_hbm.at[rows], leaf_v.at[rows], leaf_sem.at[c])

    def lev_load(l):
        return pltpu.make_async_copy(lev_hbm.at[l], lev_v.at[l], lev_sem.at[l])

    def lat_load():
        return pltpu.make_async_copy(lat_hbm, lat_v, lat_sem.at[0])

    def t_store(c):
        rows = pl.ds(pl.multiple_of(c * 128, 128), 128)
        return pltpu.make_async_copy(t_v.at[:, rows, :], t_hbm.at[:, rows, :], t_sem.at[c])

    def level_copy(l, c):
        rows = pl.ds(c * PAIRS, PAIRS)
        return pltpu.make_async_remote_copy(
            src_ref=send.at[l, rows],
            dst_ref=recv.at[l, rows],
            send_sem=l_ssem.at[l, c],
            recv_sem=l_rsem.at[l, c],
            device_id={"deg": me_d ^ (1 << l)},
            device_id_type=MESH,
        )

    def wave_copy(c, d, arriving=False):
        target = lax.rem(me_w + d, WAVE)
        place = lax.rem(me_w + WAVE - d, WAVE) if arriving else me_w
        return pltpu.make_async_remote_copy(
            src_ref=a_send.at[c, target],
            dst_ref=a_recv.at[c, place],
            send_sem=a_ssem.at[c, d - 1],
            recv_sem=a_rsem.at[c, d - 1],
            device_id={"wave": target},
            device_id_type=MESH,
        )

    for c in range(CHUNKS):
        spec_load(c).start()
        leaf_load(c).start()
    for l in range(LEVELS):
        lev_load(l).start()
    lat_load().start()

    barrier = pltpu.get_barrier_semaphore()
    for l in range(LEVELS):
        pl.semaphore_signal(barrier, inc=1, device_id={"deg": me_d ^ (1 << l)}, device_id_type=MESH)
    for d in range(1, WAVE):
        pl.semaphore_signal(
            barrier, inc=1, device_id={"wave": lax.rem(me_w + d, WAVE)}, device_id_type=MESH
        )

    def pack(l, c):
        s = lax.rem(me_d // (1 << l), 2)
        mask = lane_half == 1 - s
        for p in range(PAIRS):
            base = c * CHUNK + 2 * p
            kept = state[base + 1 - s]
            moved = pltpu.roll(state[base + s], NODE // 2, 1)
            send[l, c * PAIRS + p] = jnp.where(mask, kept, moved)

    def leaf(c):
        spec_load(c).wait()
        leaf_load(c).wait()
        degree = lax.broadcasted_iota(jnp.int32, (256, NODE), 0)
        for j in range(CHUNK):
            m = c * CHUNK + j
            coef = spec_v[m]
            picks = jnp.where(degree == skel_ref[pl.ds(m, 1), :], 1.0, 0.0).astype(jnp.bfloat16)
            acc = jnp.dot(coef, picks, preferred_element_type=jnp.float32)
            acc = acc + jnp.dot(coef, leaf_v[m], preferred_element_type=jnp.float32)
            state[m] = acc.astype(jnp.bfloat16)
        pack(0, c)

    def combine(l, c):
        level_copy(l, c).wait_recv()
        s = lax.rem(me_d // (1 << l), 2)
        mask = lane_half == s
        for p in range(PAIRS):
            base = c * CHUNK + 2 * p
            got = recv[l, c * PAIRS + p]
            turned = pltpu.roll(got, NODE // 2, 1)
            for m, other in ((base + 1 - s, got), (base + s, turned)):
                joined = jnp.where(mask, state[m], other)
                state[m] = jnp.dot(
                    joined, lev_v[l, m], preferred_element_type=jnp.float32
                ).astype(jnp.bfloat16)

    def latitudes(c):
        for j in range(CHUNK):
            m = c * CHUNK + j
            rows = jnp.dot(state[m], lat_v[m], preferred_element_type=jnp.float32)
            for r in range(2):
                lat32[pl.ds(r * CHUNK + j, 32, stride=2 * CHUNK), :] = rows[r * 32 : (r + 1) * 32]
        for w in range(WAVE):
            a_send[c, w] = lat32[w * 64 : (w + 1) * 64, :].astype(jnp.bfloat16)
        a_recv[c, me_w] = a_send[c, me_w]
        for d in range(1, WAVE):
            wave_copy(c, d).start()

    def gathered(c):
        for d in range(1, WAVE):
            wave_copy(c, d, True).wait_recv()
        for f in range(4):
            block = a_recv[c, :, f * 16 : (f + 1) * 16, :].reshape(NODE, 128)
            xt_ref[f * 128 : (f + 1) * 128, pl.ds(pl.multiple_of(c * 128, 128), 128)] = (
                block.astype(jnp.float32).T.astype(jnp.bfloat16)
            )

    def table(c):
        lanes = lax.broadcasted_iota(jnp.int32, (CHUNK, 128), 1)
        unit = 2.0 * jnp.pi / NLON
        start, turn = [], []
        for w in range(WAVE):
            q = q_v[pl.ds(pl.multiple_of(w * SLOTS + c * CHUNK, 8), CHUNK), :]
            weight = jnp.where(q == 0.0, 1.0, 2.0)
            qi = q.astype(jnp.int32)
            first = lax.rem(qi * lanes, NLON).astype(jnp.float32) * unit
            step = lax.rem(qi * 128, NLON).astype(jnp.float32) * unit
            start += [weight * jnp.cos(first), -weight * jnp.sin(first)]
            turn += [jnp.cos(step), jnp.sin(step)]

        def tile(t, carry):
            carry = list(carry)
            for half in range(2):
                for w in range(WAVE):
                    co, si = carry[2 * w], carry[2 * w + 1]
                    rc, rs = turn[2 * w], turn[2 * w + 1]
                    rows = pl.ds(pl.multiple_of(c * 128 + w * 16, 16), 16)
                    t_v[t, rows, half * 128 : (half + 1) * 128] = jnp.concatenate(
                        [co, si], axis=0
                    ).astype(jnp.bfloat16)
                    carry[2 * w] = co * rc + si * rs
                    carry[2 * w + 1] = si * rc - co * rs
            return tuple(carry)

        lax.fori_loop(0, LON_TILES, tile, tuple(start))
        t_store(c).start()

    leaf(0)
    for g in range(4):
        row = wm_ref[g : g + 1, :].astype(jnp.float32)
        q_v[g * 128 : (g + 1) * 128, :] = jnp.broadcast_to(row, (128, 128)).T
    pl.semaphore_wait(barrier, LEVELS + WAVE - 1)
    level_copy(0, 0).start()

    offsets = [0]
    for d in DELAY:
        offsets.append(offsets[-1] + d)

    def active(t, k):
        return jnp.logical_and(t >= offsets[k], t < offsets[k] + CHUNKS)

    def step(t, _):
        @pl.when(jnp.logical_and(t >= 1, t < CHUNKS))
        def _():
            leaf(t)
            level_copy(0, t).start()

        @pl.when(active(t, 1))
        def _():
            c = t - offsets[1]

            @pl.when(c == 0)
            def _():
                lev_load(0).wait()

            combine(0, c)
            pack(1, c)
            level_copy(1, c).start()

        @pl.when(active(t, 2))
        def _():
            c = t - offsets[2]

            @pl.when(c == 0)
            def _():
                lev_load(1).wait()

            combine(1, c)
            pack(2, c)
            level_copy(2, c).start()

        @pl.when(active(t, 3))
        def _():
            c = t - offsets[3]

            @pl.when(c == 0)
            def _():
                lev_load(2).wait()
                lat_load().wait()

            combine(2, c)
            latitudes(c)

        @pl.when(active(t, 4))
        def _():
            gathered(t - offsets[4])

        @pl.when(t < CHUNKS)
        def _():
            table(t)

        return 0

    lax.fori_loop(0, CHUNKS + offsets[4], step, 0)

    def drain(c, _):
        for l in range(LEVELS):
            level_copy(l, c).wait_send()
        for d in range(1, WAVE):
            wave_copy(c, d).wait_send()
        t_store(c).wait()
        return 0

    lax.fori_loop(0, CHUNKS, drain, 0)


def dft_kernel(tiles, xt_ref, t_ref, out_ref):
    for b in range(tiles):
        out_ref[:, b * LON_TILE : (b + 1) * LON_TILE] = jnp.dot(
            xt_ref[...], t_ref[b], preferred_element_type=jnp.float32
        ).astype(jnp.bfloat16)


def body(spectrum, leaf_map, level_maps, lat_map, skeleton, wavemap):
    any_spec = pl.BlockSpec(memory_space=pl.ANY)
    vmem_spec = pl.BlockSpec(memory_space=pltpu.VMEM)
    bf16, f32 = jnp.bfloat16, jnp.float32
    dma = pltpu.SemaphoreType.DMA
    xt, table = pl.pallas_call(
        comm_kernel,
        out_shape=(
            jax.ShapeDtypeStruct((512, 1024), bf16),
            jax.ShapeDtypeStruct((LON_TILES, 1024, LON_TILE), bf16),
        ),
        in_specs=[any_spec] * 4 + [vmem_spec] * 2,
        out_specs=(vmem_spec, any_spec),
        scratch_shapes=[
            pltpu.VMEM((SLOTS, COLS, 256), bf16),
            pltpu.VMEM((SLOTS, 256, NODE), bf16),
            pltpu.VMEM((LEVELS, SLOTS, NODE, NODE), bf16),
            pltpu.VMEM((SLOTS, NODE, NODE), bf16),
            pltpu.VMEM((SLOTS, COLS, NODE), bf16),
            pltpu.VMEM((LEVELS, SLOTS // 2, COLS, NODE), bf16),
            pltpu.VMEM((LEVELS, SLOTS // 2, COLS, NODE), bf16),
            pltpu.VMEM((CHUNK * COLS, NODE), f32),
            pltpu.VMEM((CHUNKS, WAVE, 64, NODE), bf16),
            pltpu.VMEM((CHUNKS, WAVE, 64, NODE), bf16),
            pltpu.VMEM((LON_TILES, 1024, LON_TILE), bf16),
            pltpu.VMEM((512, 128), f32),
            dma((CHUNKS,)),
            dma((CHUNKS,)),
            dma((LEVELS,)),
            dma((1,)),
            dma((CHUNKS,)),
            dma((LEVELS, CHUNKS)),
            dma((LEVELS, CHUNKS)),
            dma((CHUNKS, WAVE - 1)),
            dma((CHUNKS, WAVE - 1)),
        ],
        compiler_params=pltpu.CompilerParams(
            collective_id=0, has_side_effects=True, vmem_limit_bytes=60 * 1024 * 1024
        ),
    )(
        spectrum.reshape(SLOTS, COLS, 256),
        leaf_map,
        level_maps,
        lat_map,
        skeleton,
        wavemap.reshape(4, 128),
    )
    tiles = 2
    grid = pl.pallas_call(
        functools.partial(dft_kernel, tiles),
        out_shape=jax.ShapeDtypeStruct((512, NLON), bf16),
        grid=(LON_TILES // tiles,),
        in_specs=[
            pl.BlockSpec((512, 1024), lambda i: (0, 0)),
            pl.BlockSpec((tiles, 1024, LON_TILE), lambda i: (i, 0, 0)),
        ],
        out_specs=pl.BlockSpec((512, tiles * LON_TILE), lambda i: (0, i)),
        compiler_params=pltpu.CompilerParams(
            dimension_semantics=("arbitrary",), vmem_limit_bytes=32 * 1024 * 1024
        ),
    )(xt, table)
    return grid.reshape(4, 128, NLON)


def solution(mesh):
    placed = (
        P("wave", None, None, "deg"),
        P("wave", "deg", None),
        P(None, "wave", "deg", None),
        P("wave", None, "deg"),
        P("wave", "deg"),
        P(),
    )
    return jax.shard_map(
        body, mesh=mesh, in_specs=placed, out_specs=P("wave", "deg", None), check_vma=False
    )
```

profile of v0, /device:TPU:1, one launch (start us, length us, event | category | flops | bytes accessed | tf_op | source)
XLA Modules:
  0.0 78.9 jit_solution(9779758066735765977)
XLA Ops:
  0.0 59.1 %shard_map.64 = (bf16[512,1024]{1,0:T(8,128)(2,1)}, bf16[32,1024,256]{2,1,0:T(8,128)(2,1)}) custom-call(bf16[64,64,256]{2,1,0:T(8,128)(2,1)} %bitcast.3, bf16[64,256,128]{2,1,0:T(8,128)(2,1)} %leaf_hbm.1, bf16[3,64,128,128]{3,2,1,0:T(8,128)(2,1)} %lev_hbm.1, bf16[64,128,128]{2,1,0:T(8,128)(2,1)} %lat_hbm.1, s32[64,128]{1,0:T(8,128)} %skel_ref.1, ...), custom_call_target="tpu_custom_call" | custom-call | tf_op jit(solution)/shard_map/pallas_call | solution.py:269
  59.1 0.0 copy-start
  59.1 5.8 %copy-done = bf16[32,1024,256]{2,1,0:T(8,128)(2,1)S(1)} copy-done((bf16[32,1024,256]{2,1,0:T(8,128)(2,1)S(1)}, bf16[32,1024,256]{2,1,0:T(8,128)(2,1)}, u32[]{:S(2)}) %copy-start) | copy-done | bytes 16777240
  64.9 0.0 copy-start.1
  64.9 1.2 %copy-done.1 = bf16[512,1024]{1,0:T(8,128)(2,1)S(1)} copy-done((bf16[512,1024]{1,0:T(8,128)(2,1)S(1)}, bf16[512,1024]{1,0:T(8,128)(2,1)}, u32[]{:S(2)}) %copy-start.1) | copy-done | bytes 1048600
  66.1 12.8 %shard_map.65 = bf16[512,8192]{1,0:T(8,128)(2,1)} custom-call(bf16[512,1024]{1,0:T(8,128)(2,1)S(1)} %copy-done.1, bf16[32,1024,256]{2,1,0:T(8,128)(2,1)S(1)} %copy-done), custom_call_target="tpu_custom_call" | custom-call | tf_op jit(solution)/shard_map/pallas_call | solution.py:312
Async XLA Ops:
  59.1 5.8 %copy-start = (bf16[32,1024,256]{2,1,0:T(8,128)(2,1)S(1)}, bf16[32,1024,256]{2,1,0:T(8,128)(2,1)}, u32[]{:S(2)}) copy-start(bf16[32,1024,256]{2,1,0:T(8,128)(2,1)} %get-tuple-element.8.t_ref) | copy-start | bytes 50331652
  64.9 1.2 %copy-start.1 = (bf16[512,1024]{1,0:T(8,128)(2,1)S(1)}, bf16[512,1024]{1,0:T(8,128)(2,1)}, u32[]{:S(2)}) copy-start(bf16[512,1024]{1,0:T(8,128)(2,1)} %get-tuple-element.7.xt_ref) | copy-start | bytes 3145732
where the time goes:
time: 79.1 us; the launch traced here: 78.9 us
  Pallas kernels  71.8 us (91%)
  local copies, waits for them, and re-layouts  6.99 us (9%)
    pallas_call x1, Pallas kernels, body(): pl.pallas_call(comm_kernel, out_shape=(jax.ShapeDtypeStruct((512, 1024),...  59.1 us
    pallas_call x1, Pallas kernels, body(): pl.pallas_call(functools.partial(dft_kernel, tiles), out_shape=jax.ShapeD...  12.8 us
    unnamed x4, local copies, waits for them, and re-layouts  6.99 us

commit v1 on v0

v1 whole, which is shorter than its diff:
```python
import jax
import jax.numpy as jnp
from jax import lax
from jax.experimental import pallas as pl
from jax.experimental.pallas import tpu as pltpu
from jax.sharding import PartitionSpec as P

NLON = 8192
LEVELS = 3
SLOTS = 64
CHUNK = 8
CHUNKS = SLOTS // CHUNK
PAIRS = CHUNK // 2
COLS = 64
NODE = 128
WAVE = 8
LON_TILE = 256
LON_TILES = NLON // 2 // LON_TILE
MESH = pl.DeviceIdType.MESH
DELAY = (3, 3, 2, 2)
UNROLL = 4
VMEM_FIRST = 54
VMEM_SECOND = 16


def comm_kernel(
    spec_hbm, leaf_hbm, lev_hbm, lat_hbm, skel_ref, wm_ref,
    xt_ref, t_ref,
    spec_v, leaf_v, lev_v, lat_v, state, send, recv, lat32, a_send, a_recv, q_v, ph_c, ph_s,
    spec_sem, leaf_sem, lev_sem, lat_sem, l_ssem, l_rsem, a_ssem, a_rsem,
):
    me_w = lax.axis_index("wave")
    me_d = lax.axis_index("deg")
    lane_half = lax.broadcasted_iota(jnp.int32, (COLS, NODE), 1) // (NODE // 2)

    def spec_load(c):
        rows = pl.ds(c * CHUNK, CHUNK)
        return pltpu.make_async_copy(spec_hbm.at[rows], spec_v.at[rows], spec_sem.at[c])

    def leaf_load(c):
        rows = pl.ds(c * CHUNK, CHUNK)
        return pltpu.make_async_copy(leaf_hbm.at[rows], leaf_v.at[rows], leaf_sem.at[c])

    def lev_load(l):
        return pltpu.make_async_copy(lev_hbm.at[l], lev_v.at[l], lev_sem.at[l])

    def lat_load():
        return pltpu.make_async_copy(lat_hbm, lat_v, lat_sem.at[0])

    def level_copy(l, c):
        rows = pl.ds(c * PAIRS, PAIRS)
        return pltpu.make_async_remote_copy(
            src_ref=send.at[l, rows],
            dst_ref=recv.at[l, rows],
            send_sem=l_ssem.at[l, c],
            recv_sem=l_rsem.at[l, c],
            device_id={"deg": me_d ^ (1 << l)},
            device_id_type=MESH,
        )

    def wave_copy(c, d, arriving=False):
        target = lax.rem(me_w + d, WAVE)
        place = lax.rem(me_w + WAVE - d, WAVE) if arriving else me_w
        return pltpu.make_async_remote_copy(
            src_ref=a_send.at[c, target],
            dst_ref=a_recv.at[c, place],
            send_sem=a_ssem.at[c, d - 1],
            recv_sem=a_rsem.at[c, d - 1],
            device_id={"wave": target},
            device_id_type=MESH,
        )

    for c in range(CHUNKS):
        spec_load(c).start()
        leaf_load(c).start()
    for l in range(LEVELS):
        lev_load(l).start()
    lat_load().start()

    barrier = pltpu.get_barrier_semaphore()
    for l in range(LEVELS):
        pl.semaphore_signal(barrier, inc=1, device_id={"deg": me_d ^ (1 << l)}, device_id_type=MESH)
    for d in range(1, WAVE):
        pl.semaphore_signal(
            barrier, inc=1, device_id={"wave": lax.rem(me_w + d, WAVE)}, device_id_type=MESH
        )

    def pack(l, c, values):
        s = lax.rem(me_d // (1 << l), 2)
        mask = lane_half == 1 - s
        upper = jnp.broadcast_to(s, (COLS, NODE)) == 1
        for p in range(PAIRS):
            even, odd = values[2 * p], values[2 * p + 1]
            kept = jnp.where(upper, even, odd)
            moved = pltpu.roll(jnp.where(upper, odd, even), NODE // 2, 1)
            send[l, c * PAIRS + p] = jnp.where(mask, kept, moved)

    def leaf(c):
        spec_load(c).wait()
        leaf_load(c).wait()
        degree = lax.broadcasted_iota(jnp.int32, (256, NODE), 0)
        values = []
        for j in range(CHUNK):
            m = c * CHUNK + j
            coef = spec_v[m]
            picks = jnp.where(degree == skel_ref[pl.ds(m, 1), :], 1.0, 0.0).astype(jnp.bfloat16)
            acc = jnp.dot(coef, picks, preferred_element_type=jnp.float32)
            acc = acc + jnp.dot(coef, leaf_v[m], preferred_element_type=jnp.float32)
            values.append(acc.astype(jnp.bfloat16))
        for j in range(CHUNK):
            state[c * CHUNK + j] = values[j]
        pack(0, c, values)

    def combine(l, c):
        level_copy(l, c).wait_recv()
        s = lax.rem(me_d // (1 << l), 2)
        mask = lane_half == s
        upper = jnp.broadcast_to(s, (COLS, NODE)) == 1
        joined = []
        for p in range(PAIRS):
            got = recv[l, c * PAIRS + p]
            turned = pltpu.roll(got, NODE // 2, 1)
            for j, other in (
                (2 * p, jnp.where(upper, got, turned)),
                (2 * p + 1, jnp.where(upper, turned, got)),
            ):
                joined.append(jnp.where(mask, state[c * CHUNK + j], other))
        values = [
            jnp.dot(joined[j], lev_v[l, c * CHUNK + j], preferred_element_type=jnp.float32).astype(
                jnp.bfloat16
            )
            for j in range(CHUNK)
        ]
        if l < LEVELS - 1:
            for j in range(CHUNK):
                state[c * CHUNK + j] = values[j]
            pack(l + 1, c, values)
        return values

    def latitudes(c, values):
        for j in range(CHUNK):
            rows = jnp.dot(values[j], lat_v[c * CHUNK + j], preferred_element_type=jnp.float32)
            real, imag = rows[:32], rows[32:]
            at = pl.ds(c * CHUNK + j, 1)
            co, si = ph_c[at, :], ph_s[at, :]
            lat32[pl.ds(j, 32, stride=2 * CHUNK), :] = real * co + imag * si
            lat32[pl.ds(CHUNK + j, 32, stride=2 * CHUNK), :] = imag * co - real * si
        for w in range(WAVE):
            a_send[c, w] = lat32[w * 64 : (w + 1) * 64, :].astype(jnp.bfloat16)
        a_recv[c, me_w] = a_send[c, me_w]
        for d in range(1, WAVE):
            wave_copy(c, d).start()

    def gathered(pair):
        for k in range(2):
            for d in range(1, WAVE):
                wave_copy(2 * pair + k, d, True).wait_recv()
        lanes = pl.ds(pl.multiple_of(pair * 128, 128), 128)
        for f in range(4):
            block = jnp.concatenate(
                [
                    a_recv[2 * pair + k, :, f * 16 : (f + 1) * 16, :].astype(jnp.float32)
                    for k in range(2)
                ],
                axis=0,
            )
            for r in range(2):
                part = block[:, r * 8 : (r + 1) * 8, :].reshape(128, 128)
                xt_ref[r, f * 128 : (f + 1) * 128, lanes] = part.T.astype(jnp.bfloat16)

    def table(c):
        lanes = lax.broadcasted_iota(jnp.int32, (CHUNK, 128), 1)
        unit = jnp.pi / NLON
        start, turn = [], []
        for w in range(WAVE):
            q = q_v[pl.ds(pl.multiple_of(w * SLOTS + c * CHUNK, 8), CHUNK), :]
            weight = jnp.where(q == 0.0, 1.0, 2.0)
            qi = q.astype(jnp.int32)
            first = lax.rem(qi * (2 * lanes + 1), 2 * NLON).astype(jnp.float32) * unit
            step = lax.rem(qi * 256, 2 * NLON).astype(jnp.float32) * unit
            start += [weight * jnp.cos(first), weight * jnp.sin(first)]
            turn += [jnp.cos(step), jnp.sin(step)]

        def tile(t, carry):
            carry = list(carry)
            for half in range(2):
                lon = slice(half * 128, (half + 1) * 128)
                for w in range(0, WAVE, 2):
                    rows = pl.ds(pl.multiple_of(c * 64 + w * 8, 16), 16)
                    for r in range(2):
                        t_ref[t, r, rows, lon] = jnp.concatenate(
                            [carry[2 * w + r], carry[2 * w + 2 + r]], axis=0
                        ).astype(jnp.bfloat16)
                for w in range(WAVE):
                    co, si = carry[2 * w], carry[2 * w + 1]
                    rc, rs = turn[2 * w], turn[2 * w + 1]
                    carry[2 * w] = co * rc - si * rs
                    carry[2 * w + 1] = si * rc + co * rs
            return tuple(carry)

        lax.fori_loop(0, LON_TILES, tile, tuple(start))

    leaf(0)
    for g in range(4):
        row = wm_ref[g : g + 1, :].astype(jnp.float32)
        q_v[g * 128 : (g + 1) * 128, :] = jnp.broadcast_to(row, (128, 128)).T
    phase = q_v[pl.ds(pl.multiple_of(me_w * SLOTS, 8), SLOTS), :] * (jnp.pi / NLON)
    ph_c[...] = jnp.cos(phase)
    ph_s[...] = jnp.sin(phase)
    pl.semaphore_wait(barrier, LEVELS + WAVE - 1)
    level_copy(0, 0).start()

    offsets = [0]
    for d in DELAY:
        offsets.append(offsets[-1] + d)

    def active(t, k):
        return jnp.logical_and(t >= offsets[k], t < offsets[k] + CHUNKS)

    def step(t, _):
        @pl.when(jnp.logical_and(t >= 1, t < CHUNKS))
        def _():
            leaf(t)
            level_copy(0, t).start()

        @pl.when(active(t, 1))
        def _():
            c = t - offsets[1]

            @pl.when(c == 0)
            def _():
                lev_load(0).wait()

            combine(0, c)
            level_copy(1, c).start()

        @pl.when(active(t, 2))
        def _():
            c = t - offsets[2]

            @pl.when(c == 0)
            def _():
                lev_load(1).wait()

            combine(1, c)
            level_copy(2, c).start()

        @pl.when(active(t, 3))
        def _():
            c = t - offsets[3]

            @pl.when(c == 0)
            def _():
                lev_load(2).wait()
                lat_load().wait()

            latitudes(c, combine(2, c))

        @pl.when(active(t, 4))
        def _():
            c = t - offsets[4]

            @pl.when(lax.rem(c, 2) == 1)
            def _():
                gathered(c // 2)

        @pl.when(t < CHUNKS)
        def _():
            table(t)

        return 0

    lax.fori_loop(0, CHUNKS + offsets[4], step, 0)

    def drain(c, _):
        for l in range(LEVELS):
            level_copy(l, c).wait_send()
        for d in range(1, WAVE):
            wave_copy(c, d).wait_send()
        return 0

    lax.fori_loop(0, CHUNKS, drain, 0)


def dft_kernel(xt_ref, t_ref, out_hbm, low, high, low_sem, high_sem):
    def copies(t, slot):
        near = pl.ds(pl.multiple_of(t * LON_TILE, LON_TILE), LON_TILE)
        far = pl.ds(pl.multiple_of((2 * LON_TILES - 1 - t) * LON_TILE, LON_TILE), LON_TILE)
        return (
            pltpu.make_async_copy(low.at[slot], out_hbm.at[:, near], low_sem.at[slot]),
            pltpu.make_async_copy(high.at[slot], out_hbm.at[:, far], high_sem.at[slot]),
        )

    mirror = 127 - lax.broadcasted_iota(jnp.int32, (512, 128), 1)

    def group(g, _):
        for k in range(UNROLL):
            t = g * UNROLL + k

            @pl.when(g > 0)
            def _():
                for copy in copies(t - UNROLL, k):
                    copy.wait()

        for k in range(UNROLL):
            t = g * UNROLL + k
            even = jnp.dot(xt_ref[0], t_ref[t, 0], preferred_element_type=jnp.float32)
            odd = jnp.dot(xt_ref[1], t_ref[t, 1], preferred_element_type=jnp.float32)
            low[k] = (even - odd).astype(jnp.bfloat16)
            total = even + odd
            for h in range(2):
                high[k, :, h * 128 : (h + 1) * 128] = jnp.take_along_axis(
                    total[:, (1 - h) * 128 : (2 - h) * 128], mirror, axis=1
                ).astype(jnp.bfloat16)
            for copy in copies(t, k):
                copy.start()
        return 0

    lax.fori_loop(0, LON_TILES // UNROLL, group, 0)
    for k in range(UNROLL):
        for copy in copies(LON_TILES - UNROLL + k, k):
            copy.wait()


def body(spectrum, leaf_map, level_maps, lat_map, skeleton, wavemap):
    any_spec = pl.BlockSpec(memory_space=pltpu.HBM)
    vmem_spec = pl.BlockSpec(memory_space=pltpu.VMEM)
    bf16, f32 = jnp.bfloat16, jnp.float32
    dma = pltpu.SemaphoreType.DMA
    xt, table = pl.pallas_call(
        comm_kernel,
        out_shape=(
            pltpu.VMEM((2, 512, 512), bf16),
            pltpu.VMEM((LON_TILES, 2, 512, LON_TILE), bf16),
        ),
        in_specs=[any_spec] * 4 + [vmem_spec] * 2,
        out_specs=(vmem_spec, vmem_spec),
        scratch_shapes=[
            pltpu.VMEM((SLOTS, COLS, 256), bf16),
            pltpu.VMEM((SLOTS, 256, NODE), bf16),
            pltpu.VMEM((LEVELS, SLOTS, NODE, NODE), bf16),
            pltpu.VMEM((SLOTS, NODE, NODE), bf16),
            pltpu.VMEM((SLOTS, COLS, NODE), bf16),
            pltpu.VMEM((LEVELS, SLOTS // 2, COLS, NODE), bf16),
            pltpu.VMEM((LEVELS, SLOTS // 2, COLS, NODE), bf16),
            pltpu.VMEM((CHUNK * COLS, NODE), f32),
            pltpu.VMEM((CHUNKS, WAVE, 64, NODE), bf16),
            pltpu.VMEM((CHUNKS, WAVE, 64, NODE), bf16),
            pltpu.VMEM((512, 128), f32),
            pltpu.VMEM((SLOTS, 128), f32),
            pltpu.VMEM((SLOTS, 128), f32),
            dma((CHUNKS,)),
            dma((CHUNKS,)),
            dma((LEVELS,)),
            dma((1,)),
            dma((LEVELS, CHUNKS)),
            dma((LEVELS, CHUNKS)),
            dma((CHUNKS, WAVE - 1)),
            dma((CHUNKS, WAVE - 1)),
        ],
        compiler_params=pltpu.CompilerParams(
            collective_id=0, has_side_effects=True, vmem_limit_bytes=VMEM_FIRST * 1024 * 1024
        ),
    )(
        spectrum.reshape(SLOTS, COLS, 256),
        leaf_map,
        level_maps,
        lat_map,
        skeleton,
        wavemap.reshape(4, 128),
    )
    grid = pl.pallas_call(
        dft_kernel,
        out_shape=jax.ShapeDtypeStruct((512, NLON), bf16),
        in_specs=[vmem_spec, vmem_spec],
        out_specs=any_spec,
        scratch_shapes=[
            pltpu.VMEM((UNROLL, 512, LON_TILE), bf16),
            pltpu.VMEM((UNROLL, 512, LON_TILE), bf16),
            dma((UNROLL,)),
            dma((UNROLL,)),
        ],
        compiler_params=pltpu.CompilerParams(vmem_limit_bytes=VMEM_SECOND * 1024 * 1024),
    )(xt, table)
    return grid.reshape(4, 128, NLON)


def solution(mesh):
    placed = (
        P("wave", None, None, "deg"),
        P("wave", "deg", None),
        P(None, "wave", "deg", None),
        P("wave", None, "deg"),
        P("wave", "deg"),
        P(),
    )
    return jax.shard_map(
        body, mesh=mesh, in_specs=placed, out_specs=P("wave", "deg", None), check_vma=False
    )
```

time: 79.1 us -> 51 us (0.64)
  Pallas kernels: 71.8 us -> 50.9 us
  local copies, waits for them, and re-layouts: 6.99 us -> 0 us
    pallas_call x2, Pallas kernels: 71.8 us -> 50.9 us  [the longest x1 42.6 us: body(): pl.pallas_call(comm_kernel, out_shape=(pltpu.VMEM((2, 512, 512), bf16), p...]
    unnamed x4 -> x0, local copies, waits for them, and re-layouts: 6.99 us -> none
where the time goes in v1:
time: 51 us; the launch traced here: 50.9 us
  Pallas kernels  50.9 us (100%)
    pallas_call x1, Pallas kernels, body(): pl.pallas_call(comm_kernel, out_shape=(pltpu.VMEM((2, 512, 512), bf16), p...  42.6 us
    pallas_call x1, Pallas kernels, body(): pl.pallas_call(dft_kernel, out_shape=jax.ShapeDtypeStruct((512, NLON), bf...  8.27 us

profile of v1, /device:TPU:1, one launch (start us, length us, event | category | flops | bytes accessed | tf_op | source)
XLA Modules:
  0.0 50.9 jit_solution(1171159260573608403)
XLA Ops:
  0.0 42.6 %shard_map.64 = (bf16[2,512,512]{2,1,0:T(8,128)(2,1)S(1)}, bf16[16,2,512,256]{3,2,1,0:T(8,128)(2,1)S(1)}) custom-call(bf16[64,64,256]{2,1,0:T(8,128)(2,1)} %bitcast.3, bf16[64,256,128]{2,1,0:T(8,128)(2,1)} %leaf_hbm.1, bf16[3,64,128,128]{3,2,1,0:T(8,128)(2,1)} %lev_hbm.1, bf16[64,128,128]{2,1,0:T(8,128)(2,1)} %lat_hbm.1, s32[64,128]{1,0:T(8,128)} %skel_ref.1, ...), custom_call_target="tpu_custom_call" | custom-call | tf_op jit(solution)/shard_map/pallas_call | solution.py:330
  42.6 8.3 %shard_map.65 = bf16[512,8192]{1,0:T(8,128)(2,1)} custom-call(bf16[2,512,512]{2,1,0:T(8,128)(2,1)S(1)} %get-tuple-element.7.xt_ref, bf16[16,2,512,256]{3,2,1,0:T(8,128)(2,1)S(1)} %get-tuple-element.8.t_ref), custom_call_target="tpu_custom_call" | custom-call | tf_op jit(solution)/shard_map/pallas_call | solution.py:372

commit v2 on v1

--- a/solution.py
+++ b/solution.py
@@ -17,15 +17,15 @@
 LON_TILE = 256
 LON_TILES = NLON // 2 // LON_TILE
 MESH = pl.DeviceIdType.MESH
-DELAY = (3, 3, 2, 2)
+DELAY = (3, 3, 2, 3)
 UNROLL = 4
-VMEM_FIRST = 54
+VMEM_FIRST = 37
 VMEM_SECOND = 16
 
 
 def comm_kernel(
     spec_hbm, leaf_hbm, lev_hbm, lat_hbm, skel_ref, wm_ref,
-    xt_ref, t_ref,
+    xt_ref, t_ref, part_ref,
     spec_v, leaf_v, lev_v, lat_v, state, send, recv, lat32, a_send, a_recv, q_v, ph_c, ph_s,
     spec_sem, leaf_sem, lev_sem, lat_sem, l_ssem, l_rsem, a_ssem, a_rsem,
 ):
@@ -148,7 +148,7 @@
         for w in range(WAVE):
             a_send[c, w] = lat32[w * 64 : (w + 1) * 64, :].astype(jnp.bfloat16)
         a_recv[c, me_w] = a_send[c, me_w]
-        for d in range(1, WAVE):
+        for d in (4, 3, 5, 2, 6, 1, 7):
             wave_copy(c, d).start()
 
     def gathered(pair):
@@ -200,6 +200,18 @@
 
         lax.fori_loop(0, LON_TILES, tile, tuple(start))
 
+    def early(at):
+        def group(g, _):
+            for k in range(UNROLL):
+                t = at + g * UNROLL + k
+                for r in range(2):
+                    part_ref[t, r] = jnp.dot(
+                        xt_ref[r, :, :256], t_ref[t, r, :256], preferred_element_type=jnp.float32
+                    )
+            return 0
+
+        lax.fori_loop(0, LON_TILES // 2 // UNROLL, group, 0)
+
     leaf(0)
     for g in range(4):
         row = wm_ref[g : g + 1, :].astype(jnp.float32)
@@ -268,6 +280,11 @@
         def _():
             table(t)
 
+        @pl.when(t == offsets[3] + CHUNKS - 1)
+        def _():
+            early(0)
+            early(LON_TILES // 2)
+
         return 0
 
     lax.fori_loop(0, CHUNKS + offsets[4], step, 0)
@@ -282,7 +299,7 @@
     lax.fori_loop(0, CHUNKS, drain, 0)
 
 
-def dft_kernel(xt_ref, t_ref, out_hbm, low, high, low_sem, high_sem):
+def dft_kernel(xt_ref, t_ref, part_ref, out_hbm, low, high, low_sem, high_sem):
     def copies(t, slot):
         near = pl.ds(pl.multiple_of(t * LON_TILE, LON_TILE), LON_TILE)
         far = pl.ds(pl.multiple_of((2 * LON_TILES - 1 - t) * LON_TILE, LON_TILE), LON_TILE)
@@ -304,8 +321,13 @@
 
         for k in range(UNROLL):
             t = g * UNROLL + k
-            even = jnp.dot(xt_ref[0], t_ref[t, 0], preferred_element_type=jnp.float32)
-            odd = jnp.dot(xt_ref[1], t_ref[t, 1], preferred_element_type=jnp.float32)
+            even, odd = (
+                part_ref[t, r]
+                + jnp.dot(
+                    xt_ref[r, :, 256:], t_ref[t, r, 256:], preferred_element_type=jnp.float32
+                )
+                for r in range(2)
+            )
             low[k] = (even - odd).astype(jnp.bfloat16)
             total = even + odd
             for h in range(2):
@@ -327,14 +349,15 @@
     vmem_spec = pl.BlockSpec(memory_space=pltpu.VMEM)
     bf16, f32 = jnp.bfloat16, jnp.float32
     dma = pltpu.SemaphoreType.DMA
-    xt, table = pl.pallas_call(
+    xt, table, part = pl.pallas_call(
         comm_kernel,
         out_shape=(
             pltpu.VMEM((2, 512, 512), bf16),
             pltpu.VMEM((LON_TILES, 2, 512, LON_TILE), bf16),
+            pltpu.VMEM((LON_TILES, 2, 512, LON_TILE), f32),
         ),
         in_specs=[any_spec] * 4 + [vmem_spec] * 2,
-        out_specs=(vmem_spec, vmem_spec),
+        out_specs=(vmem_spec,) * 3,
         scratch_shapes=[
             pltpu.VMEM((SLOTS, COLS, 256), bf16),
             pltpu.VMEM((SLOTS, 256, NODE), bf16),
@@ -372,7 +395,7 @@
     grid = pl.pallas_call(
         dft_kernel,
         out_shape=jax.ShapeDtypeStruct((512, NLON), bf16),
-        in_specs=[vmem_spec, vmem_spec],
+        in_specs=[vmem_spec] * 3,
         out_specs=any_spec,
         scratch_shapes=[
             pltpu.VMEM((UNROLL, 512, LON_TILE), bf16),
@@ -381,7 +404,7 @@
             dma((UNROLL,)),
         ],
         compiler_params=pltpu.CompilerParams(vmem_limit_bytes=VMEM_SECOND * 1024 * 1024),
-    )(xt, table)
+    )(xt, table, part)
     return grid.reshape(4, 128, NLON)
 
 

time: 51 us -> 48.6 us (0.953)
  Pallas kernels: 50.9 us -> 48.5 us
    pallas_call x1, Pallas kernels: 8.27 us -> 6.52 us  [body(): pl.pallas_call(dft_kernel, out_shape=jax.ShapeDtypeStruct((512, NLON), bf...]
    pallas_call x1, Pallas kernels: 42.6 us -> 41.9 us  [body(): pl.pallas_call(comm_kernel, out_shape=(pltpu.VMEM((2, 512, 512), bf16), p...]
where the time goes in v2:
time: 48.6 us; the launch traced here: 48.5 us
  Pallas kernels  48.5 us (100%)
    pallas_call x1, Pallas kernels, body(): pl.pallas_call(comm_kernel, out_shape=(pltpu.VMEM((2, 512, 512), bf16), p...  41.9 us
    pallas_call x1, Pallas kernels, body(): pl.pallas_call(dft_kernel, out_shape=jax.ShapeDtypeStruct((512, NLON), bf...  6.52 us

profile of v2, /device:TPU:1, one launch (start us, length us, event | category | flops | bytes accessed | tf_op | source)
XLA Modules:
  0.0 48.5 jit_solution(4707072253646174989)
XLA Ops:
  0.0 41.9 %shard_map.64 = (bf16[2,512,512]{2,1,0:T(8,128)(2,1)S(1)}, bf16[16,2,512,256]{3,2,1,0:T(8,128)(2,1)S(1)}, f32[16,2,512,256]{3,2,1,0:T(8,128)S(1)}) custom-call(bf16[64,64,256]{2,1,0:T(8,128)(2,1)} %bitcast.3, bf16[64,256,128]{2,1,0:T(8,128)(2,1)} %leaf_hbm.1, bf16[3,64,128,128]{3,2,1,0:T(8,128)(2,1)} %lev_hbm.1, bf16[64,128,128]{2,1,0:T(8,128)(2,1)} %lat_hbm.1, ...), custom_call_target="tpu_custom_call" | custom-call | tf_op jit(solution)/shard_map/pallas_call | solution.py:352
  41.9 6.5 %shard_map.65 = bf16[512,8192]{1,0:T(8,128)(2,1)} custom-call(bf16[2,512,512]{2,1,0:T(8,128)(2,1)S(1)} %get-tuple-element.8.xt_ref, bf16[16,2,512,256]{3,2,1,0:T(8,128)(2,1)S(1)} %get-tuple-element.9.t_ref, f32[16,2,512,256]{3,2,1,0:T(8,128)S(1)} %get-tuple-element.10.part_ref), custom_call_target="tpu_custom_call" | custom-call | tf_op jit(solution)/shard_map/pallas_call | solution.py:395

commit v3 on v2

--- a/solution.py
+++ b/solution.py
@@ -18,7 +18,8 @@
 LON_TILES = NLON // 2 // LON_TILE
 MESH = pl.DeviceIdType.MESH
 DELAY = (3, 3, 2, 3)
-UNROLL = 4
+UNROLL = 16
+EARLY = 4
 VMEM_FIRST = 37
 VMEM_SECOND = 16
 
@@ -202,15 +203,15 @@
 
     def early(at):
         def group(g, _):
-            for k in range(UNROLL):
-                t = at + g * UNROLL + k
+            for k in range(EARLY):
+                t = at + g * EARLY + k
                 for r in range(2):
                     part_ref[t, r] = jnp.dot(
                         xt_ref[r, :, :256], t_ref[t, r, :256], preferred_element_type=jnp.float32
                     )
             return 0
 
-        lax.fori_loop(0, LON_TILES // 2 // UNROLL, group, 0)
+        lax.fori_loop(0, LON_TILES // 2 // EARLY, group, 0)
 
     leaf(0)
     for g in range(4):

time: 48.6 us -> 46 us (0.947)
  Pallas kernels: 48.5 us -> 45.8 us
    pallas_call x1, Pallas kernels: 6.52 us -> 3.85 us  [body(): pl.pallas_call(dft_kernel, out_shape=jax.ShapeDtypeStruct((512, NLON), bf...]
where the time goes in v3:
time: 46 us; the launch traced here: 45.8 us
  Pallas kernels  45.8 us (100%)
    pallas_call x1, Pallas kernels, body(): pl.pallas_call(comm_kernel, out_shape=(pltpu.VMEM((2, 512, 512), bf16), p...  41.9 us
    pallas_call x1, Pallas kernels, body(): pl.pallas_call(dft_kernel, out_shape=jax.ShapeDtypeStruct((512, NLON), bf...  3.85 us

profile of v3, /device:TPU:1, one launch (start us, length us, event | category | flops | bytes accessed | tf_op | source)
XLA Modules:
  0.0 45.8 jit_solution(15725606469519585060)
XLA Ops:
  0.0 41.9 %shard_map.64 = (bf16[2,512,512]{2,1,0:T(8,128)(2,1)S(1)}, bf16[16,2,512,256]{3,2,1,0:T(8,128)(2,1)S(1)}, f32[16,2,512,256]{3,2,1,0:T(8,128)S(1)}) custom-call(bf16[64,64,256]{2,1,0:T(8,128)(2,1)} %bitcast.3, bf16[64,256,128]{2,1,0:T(8,128)(2,1)} %leaf_hbm.1, bf16[3,64,128,128]{3,2,1,0:T(8,128)(2,1)} %lev_hbm.1, bf16[64,128,128]{2,1,0:T(8,128)(2,1)} %lat_hbm.1, ...), custom_call_target="tpu_custom_call" | custom-call | tf_op jit(solution)/shard_map/pallas_call | solution.py:353
  41.9 3.8 %shard_map.65 = bf16[512,8192]{1,0:T(8,128)(2,1)} custom-call(bf16[2,512,512]{2,1,0:T(8,128)(2,1)S(1)} %get-tuple-element.8.xt_ref, bf16[16,2,512,256]{3,2,1,0:T(8,128)(2,1)S(1)} %get-tuple-element.9.t_ref, f32[16,2,512,256]{3,2,1,0:T(8,128)S(1)} %get-tuple-element.10.part_ref), custom_call_target="tpu_custom_call" | custom-call | tf_op jit(solution)/shard_map/pallas_call | solution.py:396

commit v4 on v3

--- a/solution.py
+++ b/solution.py
@@ -17,7 +17,7 @@
 LON_TILE = 256
 LON_TILES = NLON // 2 // LON_TILE
 MESH = pl.DeviceIdType.MESH
-DELAY = (3, 3, 2, 3)
+DELAY = (2, 3, 2, 3)
 UNROLL = 16
 EARLY = 4
 VMEM_FIRST = 37
@@ -148,9 +148,9 @@
             lat32[pl.ds(CHUNK + j, 32, stride=2 * CHUNK), :] = imag * co - real * si
         for w in range(WAVE):
             a_send[c, w] = lat32[w * 64 : (w + 1) * 64, :].astype(jnp.bfloat16)
-        a_recv[c, me_w] = a_send[c, me_w]
         for d in (4, 3, 5, 2, 6, 1, 7):
             wave_copy(c, d).start()
+        a_recv[c, me_w] = a_send[c, me_w]
 
     def gathered(pair):
         for k in range(2):

time: 46 us -> 45.8 us (level)
  no operation moved by 1% of the time
where the time goes in v4:
time: 45.8 us; the launch traced here: 45.7 us
  Pallas kernels  45.7 us (100%)
    pallas_call x1, Pallas kernels, body(): pl.pallas_call(comm_kernel, out_shape=(pltpu.VMEM((2, 512, 512), bf16), p...  41.8 us
    pallas_call x1, Pallas kernels, body(): pl.pallas_call(dft_kernel, out_shape=jax.ShapeDtypeStruct((512, NLON), bf...  3.85 us

profile of v4, /device:TPU:1, one launch (start us, length us, event | category | flops | bytes accessed | tf_op | source)
XLA Modules:
  0.0 45.7 jit_solution(10777482437283913188)
XLA Ops:
  0.0 41.8 %shard_map.64 = (bf16[2,512,512]{2,1,0:T(8,128)(2,1)S(1)}, bf16[16,2,512,256]{3,2,1,0:T(8,128)(2,1)S(1)}, f32[16,2,512,256]{3,2,1,0:T(8,128)S(1)}) custom-call(bf16[64,64,256]{2,1,0:T(8,128)(2,1)} %bitcast.3, bf16[64,256,128]{2,1,0:T(8,128)(2,1)} %leaf_hbm.1, bf16[3,64,128,128]{3,2,1,0:T(8,128)(2,1)} %lev_hbm.1, bf16[64,128,128]{2,1,0:T(8,128)(2,1)} %lat_hbm.1, ...), custom_call_target="tpu_custom_call" | custom-call | tf_op jit(solution)/shard_map/pallas_call | solution.py:353
  41.8 3.8 %shard_map.65 = bf16[512,8192]{1,0:T(8,128)(2,1)} custom-call(bf16[2,512,512]{2,1,0:T(8,128)(2,1)S(1)} %get-tuple-element.8.xt_ref, bf16[16,2,512,256]{3,2,1,0:T(8,128)(2,1)S(1)} %get-tuple-element.9.t_ref, f32[16,2,512,256]{3,2,1,0:T(8,128)S(1)} %get-tuple-element.10.part_ref), custom_call_target="tpu_custom_call" | custom-call | tf_op jit(solution)/shard_map/pallas_call | solution.py:396
